TPU v7x, 128 devices: a whole 4x4x4 slice. The times are simulated.
128 devices in a mesh: blk: 8 (over y, z_lo), mode: 16 (over z_hi, x, core).
Axes of the slice: x: 4, y: 4, z: 4 (z_hi: 2, z_lo: 2; z = z_hi * 2 + z_lo), core: 2. Of those that a mesh axis runs over, the one named last changes fastest.
Arguments:
- density: bfloat16 [2, 256, 2048, 256], P(None, 'mode', 'blk'), may hold values from -6 to 6
- kernel_tiles: bfloat16 [256, 16, 8, 2, 128, 128], P('mode', 'blk'), may hold values from -0.125 to 0.125
- tile_index: int32 [256, 16, 8], P('mode', 'blk'), may hold values from 0 to 1
- coupling: bfloat16 [2, 9, 256, 2048], P(None, None, 'mode', 'blk'), may hold values from -4 to 4
- spread: int32 [2048], P('blk'), may hold values from 0 to 4
- liner: int32 [2048], P('blk'), may hold values 0 or 1
Outputs:
- applied: bfloat16 [2, 256, 2048, 256], P(None, 'mode', 'blk')
Inputs may be any that keep to these rules, and one draw needn't show every extreme that they name: `tile_index`: each retained tile names one column tile of its source shard.
All inputs are finite; a program needn't handle non-finite values. No bound on the sum of `liner` on one device may be relied on, other than what follows from the above.
Results may differ from a plain program's by a relative error of at most 0.0033.
Values may be sent and summed in bfloat16 or wider, within the bound.
No kernel may reach another device: no remote copies, remote signals or barrier semaphores. Data moves between devices by JAX's collectives and lax.ppermute only.
A program may use at most 320 MiB of HBM per device.

v0:
```python
import jax
import jax.numpy as jnp
from jax import lax
from jax.sharding import PartitionSpec as P


def with_halo(block, sides, width):
    for axis, dim in sides:
        count = lax.axis_size(axis)
        forward = [(i, i + 1) for i in range(count - 1)]
        backward = [(target, source) for source, target in forward]
        low = lax.ppermute(
            lax.slice_in_dim(block, block.shape[dim] - width, None, axis=dim), axis, forward
        )
        high = lax.ppermute(lax.slice_in_dim(block, 0, width, axis=dim), axis, backward)
        block = jnp.concatenate([low, block, high], axis=dim)
    return block


def tile_product(left, right):
    return jnp.einsum("mtqk,mtkr->mtqr", left, right, preferred_element_type=jnp.float32)


def couple_modes(padded, weights, mode_count):
    band_count = weights.shape[1]
    real_part = jnp.zeros((mode_count,) + padded.shape[2:], jnp.float32)
    imag_part = jnp.zeros((mode_count,) + padded.shape[2:], jnp.float32)
    for offset in range(band_count):
        shifted = padded[:, offset : offset + mode_count].astype(jnp.float32)
        weight_now = weights[:, offset].astype(jnp.float32)[..., None]
        real_part = real_part + weight_now[0] * shifted[0] - weight_now[1] * shifted[1]
        imag_part = imag_part + weight_now[0] * shifted[1] + weight_now[1] * shifted[0]
    return jnp.stack([real_part, imag_part]).astype(jnp.bfloat16)


def shards(density, kernel_tiles, tile_index, coupling, spread, liner):
    mode_count = density.shape[1]
    point_count = density.shape[2]
    rhs_count = density.shape[3]
    tile_size = kernel_tiles.shape[-1]
    row_tiles = kernel_tiles.shape[1]
    per_shard = point_count // tile_size
    band_count = coupling.shape[1]
    reach = band_count // 2
    column_ids = jnp.arange(per_shard, dtype=jnp.int32)
    initial = jnp.zeros((2, mode_count, row_tiles, tile_size, rhs_count), jnp.float32)
    gathered = lax.all_gather(density, "blk", axis=2, tiled=True)
    shard_count = gathered.shape[2] // point_count

    def one_shard(position, running):
        shard_block = lax.dynamic_slice_in_dim(gathered, position * point_count, point_count, 2)
        shard_block = shard_block.reshape(2, mode_count, per_shard, tile_size, rhs_count)
        chosen_tiles = lax.dynamic_index_in_dim(tile_index, position, 2, keepdims=False)
        one_hot = (chosen_tiles[:, :, None] == column_ids).astype(jnp.bfloat16)
        picked_tiles = jnp.einsum(
            "mts,cmsqr->cmtqr", one_hot, shard_block, preferred_element_type=jnp.float32
        ).astype(jnp.bfloat16)
        kernel_block = lax.dynamic_index_in_dim(kernel_tiles, position, 2, keepdims=False)
        real_part = tile_product(kernel_block[:, :, 0], picked_tiles[0]) - tile_product(
            kernel_block[:, :, 1], picked_tiles[1]
        )
        imag_part = tile_product(kernel_block[:, :, 0], picked_tiles[1]) + tile_product(
            kernel_block[:, :, 1], picked_tiles[0]
        )
        return running + jnp.stack([real_part, imag_part])

    near = lax.fori_loop(0, shard_count, one_shard, initial)
    near = near.reshape(2, mode_count, point_count, rhs_count)
    offsets = jnp.abs(jnp.arange(band_count, dtype=jnp.int32) - reach)
    within = (offsets[:, None] <= spread[None, :]) & (liner[None, :] == 1)
    weights = coupling * within[None, :, None, :].astype(jnp.bfloat16)
    extended = with_halo(density, (("mode", 1),), reach)
    coupled = couple_modes(extended, weights, mode_count)
    total = 0.5 * density.astype(jnp.float32) + near + coupled.astype(jnp.float32)
    return total.astype(jnp.bfloat16)


def solution(mesh):
    return jax.shard_map(
        shards,
        mesh=mesh,
        in_specs=(
            P(None, "mode", "blk", None),
            P("mode", "blk", None, None, None, None),
            P("mode", "blk", None),
            P(None, None, "mode", "blk"),
            P("blk"),
            P("blk"),
        ),
        out_specs=P(None, "mode", "blk", None),
        check_vma=False,
    )
```

profile of v0, /device:TPU:1, one launch (start us, length us, event | category | flops | bytes accessed | tf_op | source)
XLA Modules:
  0.0 1023.9 jit_solution(228144644666771216)
XLA Ops:
  7.3 3.1 fusion.14
  10.3 4.5 collective-permute-start
  17.0 9.9 collective-permute-done
  26.9 7.9 constant_dynamic-update-slice_fusion
  37.2 11.7 %slice_convert_fusion.3 = (f32[2,16,256,256]{3,2,1,0:T(8,128)}, f32[2,16,256,256]{3,2,1,0:T(8,128)}, f32[2,16,256,256]{3,2,1,0:T(8,128)}, f32[2,16,256,256]{3,2,1,0:T(8,128)}) fusion(bf16[2,20,256,256]{3,2,1,0:T(8,128)(2,1)S(1)} %constant_dynamic-update-slice_fusion.2), kind=kLoop, calls=%fused_computation.30 | loop fusion | flops 8388608 | bytes 50331648 | tf_op jit(solution)/shard_map/convert_element_type | solution.py:29
  48.9 15.3 %slice_convert_fusion.7 = (f32[2,16,256,256]{3,2,1,0:T(8,128)}, f32[2,16,256,256]{3,2,1,0:T(8,128)}, f32[2,16,256,256]{3,2,1,0:T(8,128)}, f32[2,16,256,256]{3,2,1,0:T(8,128)}) fusion(bf16[2,20,256,256]{3,2,1,0:T(8,128)(2,1)} %copy-done), kind=kLoop, calls=%fused_computation.34 | loop fusion | flops 8388608 | bytes 50331648 | tf_op jit(solution)/shard_map/convert_element_type | solution.py:29
  64.2 24.6 %subtract_convert_fusion = bf16[1,16,256,256]{3,2,1,0:T(8,128)(2,1)} fusion(f32[2,16,256,256]{3,2,1,0:T(8,128)} %get-tuple-element.162, f32[2,16,256,256]{3,2,1,0:T(8,128)} %get-tuple-element.163, f32[2,16,256,256]{3,2,1,0:T(8,128)} %get-tuple-element.164, f32[2,16,256,256]{3,2,1,0:T(8,128)} %get-tuple-element.161, ...), kind=kLoop, calls=%fused_computation.36 | loop fusion | flops 37748736 | bytes 77889536 | tf_op jit(solution)/shard_map/convert
  88.8 25.0 %add_convert_fusion = bf16[1,16,256,256]{3,2,1,0:T(8,128)(2,1)} fusion(f32[2,16,256,256]{3,2,1,0:T(8,128)} %get-tuple-element.162, f32[2,16,256,256]{3,2,1,0:T(8,128)} %get-tuple-element.163, f32[2,16,256,256]{3,2,1,0:T(8,128)} %get-tuple-element.164, f32[2,16,256,256]{3,2,1,0:T(8,128)} %get-tuple-element.161, f32[2,16,256,256]{3,2,1,0:T(8,128)} %get-tuple-element.166, ...), kind=kLoop, calls=%fused_computation.35 | loop fusion | flops 37748736 | bytes 77889536 | tf_op jit(solution)/shard_map/convert.1
  113.8 548.6 %all-gather.2.cloned.1.call-done = bf16[2,16,2048,256]{3,2,1,0:T(8,128)(2,1)} async-done(((bf16[2,16,256,256]{3,2,1,0:T(8,128)(2,1)}), bf16[2,16,2048,256]{3,2,1,0:T(8,128)(2,1)}) %all-gather.2.cloned.1.call-update) | async-done | bytes 33554448 | tf_op jit(solution)/shard_map/all_gather | solution.py:47
  662.4 346.8 %while.14 = (s32[]{:T(128)}, f32[2,16,2,128,256]{4,3,2,1,0:T(8,128)}, bf16[16,2,8,2,128,128]{5,4,3,2,1,0:T(8,128)(2,1)}, bf16[2,16,2048,256]{3,2,1,0:T(8,128)(2,...) while((s32[]{:T(128)}, f32[2,16,2,128,256]{4,3,2,1,0:T(8,128)}, ...), condition=%wide.region_1.2_spmd.clone, body=%wide.region_0.1_spmd.clone.sunk | while | flops 1092616192 | bytes 92275992 | solution.py:67
  662.4 4.8 constant_dynamic-slice_fusion.8
  667.9 16.7 %fusion.28 = bf16[2,16,2,128,256]{4,2,3,0,1:T(2,128)(2,1)S(1)} fusion(bf16[2,16,2,128,256]{4,3,2,1,0:T(8,128)(2,1)} %bitcast.95, s32[16,2]{1,0:T(8,128)S(1)} %copy.49), kind=kOutput, calls=%fused_computation.3.clone.1 | convolution fusion | flops 10485824 | bytes 8388736 | tf_op jit(solution)/shard_map/while/body/eval_jaxpr/mts,cmsqr->cmtqr/dot_general | solution.py:55
  684.7 3.0 slice_bitcast_fusion.35
  696.2 6.3 maximum_add_fusion.2
  702.5 4.6 constant_dynamic-slice_fusion.8
  707.9 16.7 %fusion.28 = bf16[2,16,2,128,256]{4,2,3,0,1:T(2,128)(2,1)S(1)} fusion(bf16[2,16,2,128,256]{4,3,2,1,0:T(8,128)(2,1)} %bitcast.95, s32[16,2]{1,0:T(8,128)S(1)} %copy.49), kind=kOutput, calls=%fused_computation.3.clone.1 | convolution fusion | flops 10485824 | bytes 8388736 | tf_op jit(solution)/shard_map/while/body/eval_jaxpr/mts,cmsqr->cmtqr/dot_general | solution.py:55
  724.7 3.0 slice_bitcast_fusion.35
  733.5 2.7 add_bitcast_fusion.2
  736.2 10.1 maximum_add_fusion.2
  746.3 4.6 constant_dynamic-slice_fusion.8
  751.7 16.7 %fusion.28 = bf16[2,16,2,128,256]{4,2,3,0,1:T(2,128)(2,1)S(1)} fusion(bf16[2,16,2,128,256]{4,3,2,1,0:T(8,128)(2,1)} %bitcast.95, s32[16,2]{1,0:T(8,128)S(1)} %copy.49), kind=kOutput, calls=%fused_computation.3.clone.1 | convolution fusion | flops 10485824 | bytes 8388736 | tf_op jit(solution)/shard_map/while/body/eval_jaxpr/mts,cmsqr->cmtqr/dot_general | solution.py:55
  768.5 3.0 slice_bitcast_fusion.35
  777.3 2.7 add_bitcast_fusion.2
  780.1 10.1 maximum_add_fusion.2
  790.1 4.6 constant_dynamic-slice_fusion.8
  795.6 16.7 %fusion.28 = bf16[2,16,2,128,256]{4,2,3,0,1:T(2,128)(2,1)S(1)} fusion(bf16[2,16,2,128,256]{4,3,2,1,0:T(8,128)(2,1)} %bitcast.95, s32[16,2]{1,0:T(8,128)S(1)} %copy.49), kind=kOutput, calls=%fused_computation.3.clone.1 | convolution fusion | flops 10485824 | bytes 8388736 | tf_op jit(solution)/shard_map/while/body/eval_jaxpr/mts,cmsqr->cmtqr/dot_general | solution.py:55
  812.3 3.0 slice_bitcast_fusion.35
  821.2 2.7 add_bitcast_fusion.2
  823.9 10.1 maximum_add_fusion.2
  833.9 4.6 constant_dynamic-slice_fusion.8
  839.4 16.7 %fusion.28 = bf16[2,16,2,128,256]{4,2,3,0,1:T(2,128)(2,1)S(1)} fusion(bf16[2,16,2,128,256]{4,3,2,1,0:T(8,128)(2,1)} %bitcast.95, s32[16,2]{1,0:T(8,128)S(1)} %copy.49), kind=kOutput, calls=%fused_computation.3.clone.1 | convolution fusion | flops 10485824 | bytes 8388736 | tf_op jit(solution)/shard_map/while/body/eval_jaxpr/mts,cmsqr->cmtqr/dot_general | solution.py:55
  856.1 3.0 slice_bitcast_fusion.35
  865.0 2.7 add_bitcast_fusion.2
  867.7 10.1 maximum_add_fusion.2
  877.8 4.6 constant_dynamic-slice_fusion.8
  883.2 16.7 %fusion.28 = bf16[2,16,2,128,256]{4,2,3,0,1:T(2,128)(2,1)S(1)} fusion(bf16[2,16,2,128,256]{4,3,2,1,0:T(8,128)(2,1)} %bitcast.95, s32[16,2]{1,0:T(8,128)S(1)} %copy.49), kind=kOutput, calls=%fused_computation.3.clone.1 | convolution fusion | flops 10485824 | bytes 8388736 | tf_op jit(solution)/shard_map/while/body/eval_jaxpr/mts,cmsqr->cmtqr/dot_general | solution.py:55
  899.9 3.0 slice_bitcast_fusion.35
  908.8 2.7 add_bitcast_fusion.2
  911.5 10.1 maximum_add_fusion.2
  921.6 4.6 constant_dynamic-slice_fusion.8
  927.0 16.7 %fusion.28 = bf16[2,16,2,128,256]{4,2,3,0,1:T(2,128)(2,1)S(1)} fusion(bf16[2,16,2,128,256]{4,3,2,1,0:T(8,128)(2,1)} %bitcast.95, s32[16,2]{1,0:T(8,128)S(1)} %copy.49), kind=kOutput, calls=%fused_computation.3.clone.1 | convolution fusion | flops 10485824 | bytes 8388736 | tf_op jit(solution)/shard_map/while/body/eval_jaxpr/mts,cmsqr->cmtqr/dot_general | solution.py:55
  943.7 3.0 slice_bitcast_fusion.35
  955.3 10.1 maximum_add_fusion.2
  965.4 4.6 constant_dynamic-slice_fusion.8
  970.8 16.7 %fusion.28 = bf16[2,16,2,128,256]{4,2,3,0,1:T(2,128)(2,1)S(1)} fusion(bf16[2,16,2,128,256]{4,3,2,1,0:T(8,128)(2,1)} %bitcast.95, s32[16,2]{1,0:T(8,128)S(1)} %copy.49), kind=kOutput, calls=%fused_computation.3.clone.1 | convolution fusion | flops 10485824 | bytes 8388736 | tf_op jit(solution)/shard_map/while/body/eval_jaxpr/mts,cmsqr->cmtqr/dot_general | solution.py:55
  987.6 3.0 slice_bitcast_fusion.35
  999.1 10.1 maximum_add_fusion.2
  1009.2 7.8 fusion.13
  (78 shorter events, 66.7 us)
Async XLA Ops:
  6.5 10.2 %copy-start.4 = (s32[256]{0:T(256)S(1)}, s32[256]{0:T(256)}, u32[]{:S(2)}) copy-start(s32[256]{0:T(256)} %param.13) | copy-start | bytes 3076
  6.5 10.3 %copy-start.3 = (s32[256]{0:T(256)S(1)}, s32[256]{0:T(256)}, u32[]{:S(2)}) copy-start(s32[256]{0:T(256)} %param.12) | copy-start | bytes 3076
  6.5 10.4 %copy-start.2 = (bf16[2,9,16,256]{3,2,1,0:T(8,128)(2,1)S(1)}, bf16[2,9,16,256]{3,2,1,0:T(8,128)(2,1)}, u32[]{:S(2)}) copy-start(bf16[2,9,16,256]{3,2,1,0:T(8,128)(2,1)} %param.11) | copy-start | bytes 442372
  6.5 655.8 %all-gather.2.cloned.1.call-start = ((), (), s32[]{:S(2)}) async-start(), calls=%async_computation | async-start | bytes 37748736 | tf_op jit(solution)/shard_map/all_gather | solution.py:47
  10.3 16.5 %collective-permute-start = (bf16[2,4,256,256]{3,2,1,0:T(8,128)(2,1)}, bf16[2,4,256,256]{3,2,1,0:T(8,128)(2,1)S(1)}, u32[]{:S(2)}, u32[]{:S(2)}) collective-permute-start(bf16[2,4,256,256]{3,2,1,0:T(8,128)(2,1)} %get-tuple-element.168), channel_id=1, source_target_pairs={{0,1},{1,2},{2,3},{3,4},{4,5},{5,6},{6,7},{7,8},{8,9},{9,10},{10,1... | collective-permute-start | bytes 3145736 | tf_op jit(solution)/shard_map/ppermute | solution.py:12
  14.8 20.1 %collective-permute-start.1 = (bf16[2,4,256,256]{3,2,1,0:T(8,128)(2,1)}, bf16[2,4,256,256]{3,2,1,0:T(8,128)(2,1)S(1)}, u32[]{:S(2)}, u32[]{:S(2)}) collective-permute-start(bf16[2,4,256,256]{3,2,1,0:T(8,128)(2,1)} %get-tuple-element.169), channel_id=1, source_target_pairs={{1,0},{2,1},{3,2},{4,3},{5,4},{6,5},{7,6},{8,7},{9,8},{10,9},{11,1... | collective-permute-start | bytes 3145736 | tf_op jit(solution)/shard_map/ppermute | solution.py:15
  34.9 2.3 copy-start
  662.4 346.8 %copy-start.1 = (bf16[1,16,256,256]{3,2,1,0:T(8,128)(2,1)S(1)}, bf16[1,16,256,256]{3,2,1,0:T(8,128)(2,1)}, u32[]{:S(2)}) copy-start(bf16[1,16,256,256]{3,2,1,0:T(8,128)(2,1)} %subtract_convert_fusion) | copy-start | bytes 6291460
Sparse Core Ops, SparseCore 0:
  9.0 653.3 all-gather.1
where the time goes:
time: 1020 us
  waiting for transfers between devices  559 us (55%)
  matrix products  188 us (18%)
  other arithmetic  169 us (17%)
  local copies, waits for them, and re-layouts  87.5 us (9%)
  between operations  13.5 us (1%)
    all_gather x1, waiting for transfers between devices, shards(): gathered = lax.all_gather(density, 'blk', axis=2, tiled=True)  549 us
    dot_general x8, matrix products, one_shard(): jnp.einsum('mts,cmsqr->cmtqr', one_hot, shard_block, preferred_element_ty...  134 us
    add x8, other arithmetic, one_shard(): return running + jnp.stack([real_part, imag_part])  76.8 us
    dot_general x32, matrix products, tile_product(): jnp.einsum('mtqk,mtkr->mtqr', left, right, preferred_element_type=jnp.flo...  54 us
    another operation x2, other arithmetic  49.6 us
    dynamic_slice x8, local copies, waits for them, and re-layouts, one_shard(): lax.dynamic_slice_in_dim(gathered, position * point_count, point_count, 2)  37.3 us
    convert_element_type x2, other arithmetic, couple_modes(): shifted = padded[:, offset:offset + mode_count].astype(jnp.float32)  27 us
    squeeze x8, local copies, waits for them, and re-layouts, one_shard(): picked_tiles[0]  23.6 us
  transfers between devices with their start and end apart: 3, of which 2 were waited for; matrix products, arithmetic and copies ran while one was open for 9% of the time, Pallas kernels for 0%

commit v1 on v0

--- a/solution.py
+++ b/solution.py
@@ -2,6 +2,13 @@
 import jax.numpy as jnp
 from jax import lax
 from jax.sharding import PartitionSpec as P
+
+
+def all_by_exchange(x, axis, dim):
+    peers = lax.axis_size(axis)
+    parts = jnp.stack([x for _ in range(peers)])
+    parts = lax.all_to_all(parts, axis, split_axis=0, concat_axis=0)
+    return jnp.concatenate(parts, axis=dim)
 
 
 def with_halo(block, sides, width):
@@ -44,7 +51,7 @@
     reach = band_count // 2
     column_ids = jnp.arange(per_shard, dtype=jnp.int32)
     initial = jnp.zeros((2, mode_count, row_tiles, tile_size, rhs_count), jnp.float32)
-    gathered = lax.all_gather(density, "blk", axis=2, tiled=True)
+    gathered = all_by_exchange(density, "blk", 2)
     shard_count = gathered.shape[2] // point_count
 
     def one_shard(position, running):

time: 1020 us -> 863 us (0.85)
  waiting for transfers between devices: 559 us -> 367 us
  local copies, waits for them, and re-layouts: 87.5 us -> 123 us
  between operations: 13.5 us -> 0.16 us
    all_gather x1 -> x0, waiting for transfers between devices: 549 us -> none  [shards(): gathered = lax.all_gather(density, 'blk', axis=2, tiled=True)]
    all_to_all x0 -> x1, waiting for transfers between devices: none -> 357 us  [all_by_exchange(): parts = lax.all_to_all(parts, axis, split_axis=0, concat_axis=0)]
    all_to_all x0 -> x1, local copies, waits for them, and re-layouts: none -> 23 us  [all_by_exchange(): parts = lax.all_to_all(parts, axis, split_axis=0, concat_axis=0)]
    another operation x0 -> x1, local copies, waits for them, and re-layouts: none -> 12.4 us  [all_by_exchange(): parts = jnp.stack([x for _ in range(peers)])]
  transfers between devices with their start and end apart: 3 -> 3, of which waited for: 2 -> 2; matrix products, arithmetic and copies ran while one was open for 9% -> 10% of each run, Pallas kernels for 0% -> 0%
where the time goes in v1:
time: 863 us; the launch traced here: 861 us
  waiting for transfers between devices  367 us (43%)
  matrix products  188 us (22%)
  other arithmetic  169 us (20%)
  local copies, waits for them, and re-layouts  123 us (14%)
  starting transfers between devices  13.5 us (2%)
    all_to_all x1, waiting for transfers between devices, all_by_exchange(): parts = lax.all_to_all(parts, axis, split_axis=0, concat_axis=0)  357 us
    dot_general x8, matrix products, one_shard(): jnp.einsum('mts,cmsqr->cmtqr', one_hot, shard_block, preferred_element_ty...  134 us
    add x8, other arithmetic, one_shard(): return running + jnp.stack([real_part, imag_part])  76.6 us
    dot_general x32, matrix products, tile_product(): jnp.einsum('mtqk,mtkr->mtqr', left, right, preferred_element_type=jnp.flo...  54.2 us
    another operation x2, other arithmetic  49.2 us
    dynamic_slice x8, local copies, waits for them, and re-layouts, one_shard(): lax.dynamic_slice_in_dim(gathered, position * point_count, point_count, 2)  37.3 us
    convert_element_type x2, other arithmetic, couple_modes(): shifted = padded[:, offset:offset + mode_count].astype(jnp.float32)  27 us
    squeeze x8, local copies, waits for them, and re-layouts, one_shard(): picked_tiles[0]  23.6 us
  transfers between devices with their start and end apart: 3, of which 2 were waited for; matrix products, arithmetic and copies ran while one was open for 10% of the time, Pallas kernels for 0%

profile of v1, /device:TPU:1, one launch (start us, length us, event | category | flops | bytes accessed | tf_op | source)
XLA Modules:
  0.0 860.8 jit_solution(11411039987848181569)
XLA Ops:
  0.0 12.4 %stack.38 = bf16[8,2,16,256,256]{4,3,2,1,0:T(8,128)(2,1)} broadcast(bf16[2,16,256,256]{3,2,1,0:T(8,128)(2,1)} %param.8), dimensions={1,2,3,4} | broadcast | bytes 37748736 | tf_op jit(solution)/shard_map/stack | solution.py:9
  12.4 7.1 all-to-all-start
  19.5 3.1 fusion.14
  22.6 4.5 collective-permute-start
  29.3 9.9 %collective-permute-done = bf16[2,4,256,256]{3,2,1,0:T(8,128)(2,1)S(1)} collective-permute-done((bf16[2,4,256,256]{3,2,1,0:T(8,128)(2,1)}, bf16[2,4,256,256]{3,2,1,0:T(8,128)(2,1)S(1)}, u32[]{:S(2)}, u32[]{:S(2)}) %collective-permute-start) | collective-permute-done | bytes 1048608 | tf_op jit(solution)/shard_map/ppermute | solution.py:19
  39.2 8.0 constant_dynamic-update-slice_fusion
  49.6 11.7 %slice_convert_fusion.3 = (f32[2,16,256,256]{3,2,1,0:T(8,128)}, f32[2,16,256,256]{3,2,1,0:T(8,128)}, f32[2,16,256,256]{3,2,1,0:T(8,128)}, f32[2,16,256,256]{3,2,1,0:T(8,128)}) fusion(bf16[2,20,256,256]{3,2,1,0:T(8,128)(2,1)S(1)} %constant_dynamic-update-slice_fusion.2), kind=kLoop, calls=%fused_computation.30 | loop fusion | flops 8388608 | bytes 50331648 | tf_op jit(solution)/shard_map/convert_element_type | solution.py:36
  61.3 15.2 %slice_convert_fusion.7 = (f32[2,16,256,256]{3,2,1,0:T(8,128)}, f32[2,16,256,256]{3,2,1,0:T(8,128)}, f32[2,16,256,256]{3,2,1,0:T(8,128)}, f32[2,16,256,256]{3,2,1,0:T(8,128)}) fusion(bf16[2,20,256,256]{3,2,1,0:T(8,128)(2,1)} %copy-done), kind=kLoop, calls=%fused_computation.34 | loop fusion | flops 8388608 | bytes 50331648 | tf_op jit(solution)/shard_map/convert_element_type | solution.py:36
  76.6 24.6 %subtract_convert_fusion = bf16[1,16,256,256]{3,2,1,0:T(8,128)(2,1)} fusion(f32[2,16,256,256]{3,2,1,0:T(8,128)} %get-tuple-element.172, f32[2,16,256,256]{3,2,1,0:T(8,128)} %get-tuple-element.173, f32[2,16,256,256]{3,2,1,0:T(8,128)} %get-tuple-element.174, f32[2,16,256,256]{3,2,1,0:T(8,128)} %get-tuple-element.171, ...), kind=kLoop, calls=%fused_computation.36 | loop fusion | flops 37748736 | bytes 77889536 | tf_op jit(solution)/shard_map/convert
  101.2 24.6 %add_convert_fusion = bf16[1,16,256,256]{3,2,1,0:T(8,128)(2,1)} fusion(f32[2,16,256,256]{3,2,1,0:T(8,128)} %get-tuple-element.172, f32[2,16,256,256]{3,2,1,0:T(8,128)} %get-tuple-element.173, f32[2,16,256,256]{3,2,1,0:T(8,128)} %get-tuple-element.174, f32[2,16,256,256]{3,2,1,0:T(8,128)} %get-tuple-element.171, f32[2,16,256,256]{3,2,1,0:T(8,128)} %get-tuple-element.176, ...), kind=kLoop, calls=%fused_computation.35 | loop fusion | flops 37748736 | bytes 77889536 | tf_op jit(solution)/shard_map/convert.1
  125.8 357.2 %all-to-all-done = bf16[8,2,16,256,256]{4,3,2,1,0:T(8,128)(2,1)} async-done(((bf16[8,2,16,256,256]{4,3,2,1,0:T(8,128)(2,1)}), bf16[8,2,16,256,256]{4,3,2,1,0:T(8,128)(2,1)}, u32[]{:S(2)}, u32[]{:S(2)}) %all-to-all-start) | async-done | bytes 33554464 | tf_op jit(solution)/shard_map/all_to_all | solution.py:10
  483.0 23.0 %copy.36 = bf16[8,2,16,256,256]{4,3,0,2,1:T(8,128)(2,1)} copy(bf16[8,2,16,256,256]{4,3,2,1,0:T(8,128)(2,1)} %all-to-all-done) | data formatting | bytes 67108864 | tf_op jit(solution)/shard_map/all_to_all | solution.py:10
  506.0 347.0 %while.14 = (s32[]{:T(128)}, f32[2,16,2,128,256]{4,3,2,1,0:T(8,128)}, bf16[16,2,8,2,128,128]{5,4,3,2,1,0:T(8,128)(2,1)}, bf16[2,16,2048,256]{3,2,1,0:T(8,128)(2,...) while((s32[]{:T(128)}, f32[2,16,2,128,256]{4,3,2,1,0:T(8,128)}, ...), condition=%wide.region_1.2_spmd.clone, body=%wide.region_0.1_spmd.clone.sunk | while | flops 1092616192 | bytes 92275992 | solution.py:74
  506.2 4.8 constant_dynamic-slice_fusion.8
  511.7 16.7 %fusion.28 = bf16[2,16,2,128,256]{4,2,3,0,1:T(2,128)(2,1)S(1)} fusion(bf16[2,16,2,128,256]{4,3,2,1,0:T(8,128)(2,1)} %bitcast.98, s32[16,2]{1,0:T(8,128)S(1)} %copy.66), kind=kOutput, calls=%fused_computation.3.clone.1 | convolution fusion | flops 10485824 | bytes 8388736 | tf_op jit(solution)/shard_map/while/body/eval_jaxpr/mts,cmsqr->cmtqr/dot_general | solution.py:62
  528.4 3.0 slice_bitcast_fusion.35
  540.0 6.2 maximum_add_fusion.2
  546.3 4.6 constant_dynamic-slice_fusion.8
  551.7 16.7 %fusion.28 = bf16[2,16,2,128,256]{4,2,3,0,1:T(2,128)(2,1)S(1)} fusion(bf16[2,16,2,128,256]{4,3,2,1,0:T(8,128)(2,1)} %bitcast.98, s32[16,2]{1,0:T(8,128)S(1)} %copy.66), kind=kOutput, calls=%fused_computation.3.clone.1 | convolution fusion | flops 10485824 | bytes 8388736 | tf_op jit(solution)/shard_map/while/body/eval_jaxpr/mts,cmsqr->cmtqr/dot_general | solution.py:62
  568.4 3.0 slice_bitcast_fusion.35
  580.0 10.1 %maximum_add_fusion.2 = f32[2,16,2,128,256]{4,3,2,1,0:T(8,128)} fusion(f32[1,16,2,128,256]{4,3,2,1,0:T(8,128)} %add_bitcast_fusion.2, f32[1,16,2,128,256]{4,3,2,1,0:T(8,128)} %subtract_bitcast_fusion.2, f32[2,16,2,128,256]{4,3,2,1,0:T(8,128)} %get-tuple-element.260, pred[]{:T(512)S(6)} %compare.3), kind=kLoop, calls=%fused_computation.1.clone.1 | loop fusion | flops 6291456 | bytes 25165824 | tf_op jit(solution)/shard_map/while/body/eval_jaxpr/add | solution.py:72
  590.1 4.6 constant_dynamic-slice_fusion.8
  595.5 16.7 %fusion.28 = bf16[2,16,2,128,256]{4,2,3,0,1:T(2,128)(2,1)S(1)} fusion(bf16[2,16,2,128,256]{4,3,2,1,0:T(8,128)(2,1)} %bitcast.98, s32[16,2]{1,0:T(8,128)S(1)} %copy.66), kind=kOutput, calls=%fused_computation.3.clone.1 | convolution fusion | flops 10485824 | bytes 8388736 | tf_op jit(solution)/shard_map/while/body/eval_jaxpr/mts,cmsqr->cmtqr/dot_general | solution.py:62
  612.2 3.0 slice_bitcast_fusion.35
  621.1 2.7 add_bitcast_fusion.2
  623.8 10.1 %maximum_add_fusion.2 = f32[2,16,2,128,256]{4,3,2,1,0:T(8,128)} fusion(f32[1,16,2,128,256]{4,3,2,1,0:T(8,128)} %add_bitcast_fusion.2, f32[1,16,2,128,256]{4,3,2,1,0:T(8,128)} %subtract_bitcast_fusion.2, f32[2,16,2,128,256]{4,3,2,1,0:T(8,128)} %get-tuple-element.260, pred[]{:T(512)S(6)} %compare.3), kind=kLoop, calls=%fused_computation.1.clone.1 | loop fusion | flops 6291456 | bytes 25165824 | tf_op jit(solution)/shard_map/while/body/eval_jaxpr/add | solution.py:72
  633.9 4.6 constant_dynamic-slice_fusion.8
  639.3 16.7 %fusion.28 = bf16[2,16,2,128,256]{4,2,3,0,1:T(2,128)(2,1)S(1)} fusion(bf16[2,16,2,128,256]{4,3,2,1,0:T(8,128)(2,1)} %bitcast.98, s32[16,2]{1,0:T(8,128)S(1)} %copy.66), kind=kOutput, calls=%fused_computation.3.clone.1 | convolution fusion | flops 10485824 | bytes 8388736 | tf_op jit(solution)/shard_map/while/body/eval_jaxpr/mts,cmsqr->cmtqr/dot_general | solution.py:62
  656.1 3.0 slice_bitcast_fusion.35
  664.9 2.7 add_bitcast_fusion.2
  667.6 10.1 %maximum_add_fusion.2 = f32[2,16,2,128,256]{4,3,2,1,0:T(8,128)} fusion(f32[1,16,2,128,256]{4,3,2,1,0:T(8,128)} %add_bitcast_fusion.2, f32[1,16,2,128,256]{4,3,2,1,0:T(8,128)} %subtract_bitcast_fusion.2, f32[2,16,2,128,256]{4,3,2,1,0:T(8,128)} %get-tuple-element.260, pred[]{:T(512)S(6)} %compare.3), kind=kLoop, calls=%fused_computation.1.clone.1 | loop fusion | flops 6291456 | bytes 25165824 | tf_op jit(solution)/shard_map/while/body/eval_jaxpr/add | solution.py:72
  677.7 4.6 constant_dynamic-slice_fusion.8
  683.1 16.7 %fusion.28 = bf16[2,16,2,128,256]{4,2,3,0,1:T(2,128)(2,1)S(1)} fusion(bf16[2,16,2,128,256]{4,3,2,1,0:T(8,128)(2,1)} %bitcast.98, s32[16,2]{1,0:T(8,128)S(1)} %copy.66), kind=kOutput, calls=%fused_computation.3.clone.1 | convolution fusion | flops 10485824 | bytes 8388736 | tf_op jit(solution)/shard_map/while/body/eval_jaxpr/mts,cmsqr->cmtqr/dot_general | solution.py:62
  699.9 3.0 slice_bitcast_fusion.35
  711.5 10.1 %maximum_add_fusion.2 = f32[2,16,2,128,256]{4,3,2,1,0:T(8,128)} fusion(f32[1,16,2,128,256]{4,3,2,1,0:T(8,128)} %add_bitcast_fusion.2, f32[1,16,2,128,256]{4,3,2,1,0:T(8,128)} %subtract_bitcast_fusion.2, f32[2,16,2,128,256]{4,3,2,1,0:T(8,128)} %get-tuple-element.260, pred[]{:T(512)S(6)} %compare.3), kind=kLoop, calls=%fused_computation.1.clone.1 | loop fusion | flops 6291456 | bytes 25165824 | tf_op jit(solution)/shard_map/while/body/eval_jaxpr/add | solution.py:72
  721.5 4.6 constant_dynamic-slice_fusion.8
  726.9 16.7 %fusion.28 = bf16[2,16,2,128,256]{4,2,3,0,1:T(2,128)(2,1)S(1)} fusion(bf16[2,16,2,128,256]{4,3,2,1,0:T(8,128)(2,1)} %bitcast.98, s32[16,2]{1,0:T(8,128)S(1)} %copy.66), kind=kOutput, calls=%fused_computation.3.clone.1 | convolution fusion | flops 10485824 | bytes 8388736 | tf_op jit(solution)/shard_map/while/body/eval_jaxpr/mts,cmsqr->cmtqr/dot_general | solution.py:62
  743.7 3.0 slice_bitcast_fusion.35
  755.3 10.1 %maximum_add_fusion.2 = f32[2,16,2,128,256]{4,3,2,1,0:T(8,128)} fusion(f32[1,16,2,128,256]{4,3,2,1,0:T(8,128)} %add_bitcast_fusion.2, f32[1,16,2,128,256]{4,3,2,1,0:T(8,128)} %subtract_bitcast_fusion.2, f32[2,16,2,128,256]{4,3,2,1,0:T(8,128)} %get-tuple-element.260, pred[]{:T(512)S(6)} %compare.3), kind=kLoop, calls=%fused_computation.1.clone.1 | loop fusion | flops 6291456 | bytes 25165824 | tf_op jit(solution)/shard_map/while/body/eval_jaxpr/add | solution.py:72
  765.3 4.6 constant_dynamic-slice_fusion.8
  770.8 16.7 %fusion.28 = bf16[2,16,2,128,256]{4,2,3,0,1:T(2,128)(2,1)S(1)} fusion(bf16[2,16,2,128,256]{4,3,2,1,0:T(8,128)(2,1)} %bitcast.98, s32[16,2]{1,0:T(8,128)S(1)} %copy.66), kind=kOutput, calls=%fused_computation.3.clone.1 | convolution fusion | flops 10485824 | bytes 8388736 | tf_op jit(solution)/shard_map/while/body/eval_jaxpr/mts,cmsqr->cmtqr/dot_general | solution.py:62
  787.5 3.0 slice_bitcast_fusion.35
  799.1 10.1 %maximum_add_fusion.2 = f32[2,16,2,128,256]{4,3,2,1,0:T(8,128)} fusion(f32[1,16,2,128,256]{4,3,2,1,0:T(8,128)} %add_bitcast_fusion.2, f32[1,16,2,128,256]{4,3,2,1,0:T(8,128)} %subtract_bitcast_fusion.2, f32[2,16,2,128,256]{4,3,2,1,0:T(8,128)} %get-tuple-element.260, pred[]{:T(512)S(6)} %compare.3), kind=kLoop, calls=%fused_computation.1.clone.1 | loop fusion | flops 6291456 | bytes 25165824 | tf_op jit(solution)/shard_map/while/body/eval_jaxpr/add | solution.py:72
  809.1 4.6 constant_dynamic-slice_fusion.8
  814.6 16.7 %fusion.28 = bf16[2,16,2,128,256]{4,2,3,0,1:T(2,128)(2,1)S(1)} fusion(bf16[2,16,2,128,256]{4,3,2,1,0:T(8,128)(2,1)} %bitcast.98, s32[16,2]{1,0:T(8,128)S(1)} %copy.66), kind=kOutput, calls=%fused_computation.3.clone.1 | convolution fusion | flops 10485824 | bytes 8388736 | tf_op jit(solution)/shard_map/while/body/eval_jaxpr/mts,cmsqr->cmtqr/dot_general | solution.py:62
  831.3 3.0 slice_bitcast_fusion.35
  842.9 10.1 %maximum_add_fusion.2 = f32[2,16,2,128,256]{4,3,2,1,0:T(8,128)} fusion(f32[1,16,2,128,256]{4,3,2,1,0:T(8,128)} %add_bitcast_fusion.2, f32[1,16,2,128,256]{4,3,2,1,0:T(8,128)} %subtract_bitcast_fusion.2, f32[2,16,2,128,256]{4,3,2,1,0:T(8,128)} %get-tuple-element.260, pred[]{:T(512)S(6)} %compare.3), kind=kLoop, calls=%fused_computation.1.clone.1 | loop fusion | flops 6291456 | bytes 25165824 | tf_op jit(solution)/shard_map/while/body/eval_jaxpr/add | solution.py:72
  853.0 7.8 fusion.13
  (79 shorter events, 74.3 us)
Async XLA Ops:
  12.4 470.6 %all-to-all-start = ((bf16[8,2,16,256,256]{4,3,2,1,0:T(8,128)(2,1)}), bf16[8,2,16,256,256]{4,3,2,1,0:T(8,128)(2,1)}, u32[]{:S(2)}, u32[]{:S(2)}) async-start(bf16[8,2,16,256,256]{4,3,2,1,0:T(8,128)(2,1)} %stack.38), calls=%async_computation | async-start | bytes 67108864 | tf_op jit(solution)/shard_map/all_to_all | solution.py:10
  19.5 9.6 %copy-start.4 = (s32[256]{0:T(256)S(1)}, s32[256]{0:T(256)}, u32[]{:S(2)}) copy-start(s32[256]{0:T(256)} %param.13) | copy-start | bytes 3076
  19.5 9.6 %copy-start.3 = (s32[256]{0:T(256)S(1)}, s32[256]{0:T(256)}, u32[]{:S(2)}) copy-start(s32[256]{0:T(256)} %param.12) | copy-start | bytes 3076
  19.5 9.7 %copy-start.2 = (bf16[2,9,16,256]{3,2,1,0:T(8,128)(2,1)S(1)}, bf16[2,9,16,256]{3,2,1,0:T(8,128)(2,1)}, u32[]{:S(2)}) copy-start(bf16[2,9,16,256]{3,2,1,0:T(8,128)(2,1)} %param.11) | copy-start | bytes 442372
  22.6 16.5 %collective-permute-start = (bf16[2,4,256,256]{3,2,1,0:T(8,128)(2,1)}, bf16[2,4,256,256]{3,2,1,0:T(8,128)(2,1)S(1)}, u32[]{:S(2)}, u32[]{:S(2)}) collective-permute-start(bf16[2,4,256,256]{3,2,1,0:T(8,128)(2,1)} %get-tuple-element.178), channel_id=1, source_target_pairs={{0,1},{1,2},{2,3},{3,4},{4,5},{5,6},{6,7},{7,8},{8,9},{9,10},{10,1... | collective-permute-start | bytes 3145736 | tf_op jit(solution)/shard_map/ppermute | solution.py:19
  27.1 20.2 %collective-permute-start.1 = (bf16[2,4,256,256]{3,2,1,0:T(8,128)(2,1)}, bf16[2,4,256,256]{3,2,1,0:T(8,128)(2,1)S(1)}, u32[]{:S(2)}, u32[]{:S(2)}) collective-permute-start(bf16[2,4,256,256]{3,2,1,0:T(8,128)(2,1)} %get-tuple-element.179), channel_id=1, source_target_pairs={{1,0},{2,1},{3,2},{4,3},{5,4},{6,5},{7,6},{8,7},{9,8},{10,9},{11,1... | collective-permute-start | bytes 3145736 | tf_op jit(solution)/shard_map/ppermute | solution.py:22
  47.2 2.3 copy-start
  506.0 347.0 %copy-start.1 = (bf16[1,16,256,256]{3,2,1,0:T(8,128)(2,1)S(1)}, bf16[1,16,256,256]{3,2,1,0:T(8,128)(2,1)}, u32[]{:S(2)}) copy-start(bf16[1,16,256,256]{3,2,1,0:T(8,128)(2,1)} %subtract_convert_fusion) | copy-start | bytes 6291460
